TPU v7x, 256 devices: a whole 4x4x8 slice. The times are simulated.
256 devices in a mesh: row: 32 (over y, x, core), col: 8 (over z).
Axes of the slice: x: 4, y: 4, z: 8, core: 2. Of those that a mesh axis runs over, the one named last changes fastest.
Arguments:
- values: float32 [4, 32, 128, 16, 8, 128], P(None, 'row', None, None, 'col'), may hold values from -6 to 6
- fill: int32 [4, 32, 16, 8], P(None, 'row', None, 'col'), may hold values 0 or 1
- inverses: float32 [2, 128, 128], replicated, may hold values from -0.06 to 0.26
- pivots: int32 [2, 128], replicated, may hold values from 0 to 127, each once within a row
Outputs:
- factored: float32 [4, 32, 128, 16, 8, 128], P(None, 'row', None, None, 'col')
Inputs may be any that keep to these rules, and one draw needn't show every extreme that they name: `pivots`: each row lists 0 to 127 once.
All inputs are finite; a program needn't handle non-finite values. No bound on the sum of `fill` on one device may be relied on, other than what follows from the above.
Results may differ from a plain program's by a relative error of at most 0.0001.
Values sent between devices are 32-bit elements; how exact they have to be, the bound alone decides.
A program may use at most 128 MiB of HBM per device.

v0:
```python
import jax
import jax.numpy as jnp
from jax import lax
from jax.sharding import PartitionSpec as P

HIGH = lax.Precision.HIGHEST


def spread(shard, axis, root):
    mine = lax.axis_index(axis) == root
    return lax.psum(jnp.where(mine, shard, jnp.zeros_like(shard)), axis)


def per_device(values, fill, inverses, pivots):
    proc_rows = lax.axis_size("row")
    proc_cols = lax.axis_size("col")
    my_row = lax.axis_index("row")
    my_col = lax.axis_index("col")
    fill_mask = fill[:, 0, :, 0].astype(jnp.float32)
    matrix = values[:, 0, :, :, 0, :] * fill_mask[:, None, :, None]
    local_rows = matrix.shape[0]
    local_cols = matrix.shape[2]
    global_rows = jnp.arange(local_rows) * proc_rows + my_row
    global_cols = jnp.arange(local_cols) * proc_cols + my_col

    def panels(matrix, step):
        row_local = step // proc_rows
        row_owner = step % proc_rows
        col_local = step // proc_cols
        col_owner = step % proc_cols
        row_blocks = matrix[row_local]
        permuted = jnp.take(row_blocks, pivots[step], axis=0)
        u_row = jnp.where((global_cols >= step)[None, :, None], permuted, row_blocks)
        matrix = matrix.at[row_local].set(jnp.where(my_row == row_owner, u_row, row_blocks))
        col_blocks = matrix[:, :, col_local, :]
        below = (global_rows > step)[:, None, None]
        right = (global_cols > step)[None, :, None]
        factored = jnp.einsum("rpm,mq->rpq", col_blocks, inverses[step], precision=HIGH)
        l_col = jnp.where(below, factored, col_blocks)
        matrix = matrix.at[:, :, col_local, :].set(
            jnp.where(my_col == col_owner, l_col, col_blocks)
        )
        l_panel = spread(jnp.where(below, factored, 0.0), "col", col_owner)
        u_panel = spread(jnp.where(right, u_row, 0.0), "row", row_owner)
        return (matrix, l_panel, u_panel)

    def trailing(matrix, l_panel, u_panel):
        update = jnp.einsum("rpm,mcq->rpcq", l_panel, u_panel, precision=HIGH)
        return matrix - fill_mask[:, None, :, None] * update

    matrix, l_first, u_first = panels(matrix, 0)
    matrix = trailing(matrix, l_first, u_first)
    matrix, l_second, u_second = panels(matrix, 1)
    matrix = trailing(matrix, l_second, u_second)
    return matrix[:, None, :, :, None, :]


def solution(mesh):
    placed = (P(None, "row", None, None, "col", None), P(None, "row", None, "col"), P(), P())
    return jax.shard_map(
        per_device,
        mesh=mesh,
        in_specs=placed,
        out_specs=P(None, "row", None, None, "col", None),
        check_vma=False,
    )
```

profile of v0, /device:TPU:13, one launch (start us, length us, event | category | flops | bytes accessed | tf_op | source)
XLA Modules:
  0.0 435.4 jit_solution(11974760747969211962)
XLA Ops:
  6.5 0.0 all-reduce.5.cloned.1.call-start
  6.6 0.7 convert_element_type.4
  7.2 3.9 bitcast_multiply_fusion
  11.2 0.0 copy-start
  11.2 2.0 copy-done
  13.2 0.0 copy-start.3
  13.2 0.1 slice_bitcast_fusion.1
  13.3 0.6 copy.17
  13.9 0.0 copy-done.3
  14.0 0.0 copy-start.2
  14.0 0.8 gather_fusion
  14.7 2.7 select_select_fusion.1
  17.5 1.4 bitcast_dynamic-update-slice_fusion.1
  18.9 0.0 copy-done.2
  18.9 2.0 select_select_fusion.5
  20.9 0.0 all-reduce.5.cloned.1.call-update
  21.0 0.0 all-reduce.7.cloned.1.call-start
  21.0 0.7 all-reduce.7.cloned.1.call-update
  21.7 0.0 all-reduce.9.cloned.1.call-start
  21.8 0.1 copy.15
  21.9 1.0 slice_bitcast_fusion.3
  22.9 0.8 fusion.5
  23.7 68.3 %all-reduce.5.cloned.1.call-done = f32[4,128,128]{2,1,0:T(8,128)} async-done(((f32[4,128,128]{2,1,0:T(8,128)}), f32[4,128,128]{2,1,0:T(8,128)}) %all-reduce.5.cloned.1.call-update) | async-done | bytes 262160 | tf_op jit(solution)/shard_map/psum | solution.py:11
  91.9 118.9 %all-reduce.7.cloned.1.call-done = f32[128,16,128]{2,0,1:T(8,128)} async-done(((f32[128,16,128]{2,0,1:T(8,128)}), f32[128,16,128]{2,0,1:T(8,128)}) %all-reduce.7.cloned.1.call-update) | async-done | bytes 1048592 | tf_op jit(solution)/shard_map/psum | solution.py:11
  210.8 6.4 %copy_subtract_fusion = f32[4,128,16,128]{3,1,0,2:T(8,128)S(1)} fusion(f32[4,128,16,128]{3,1,2,0:T(8,128)} %fusion.5, f32[4,16]{0,1:T(8,128)S(1)} %copy.15, f32[128,16,128]{2,0,1:T(8,128)} %all-reduce.7.cloned.1.call-done, f32[4,128,128]{2,1,0:T(8,128)} %all-reduce.5.cloned.1.call-done), kind=kOutput, calls=%fused_computation.3 | convolution fusion | flops 1612709888 | bytes 9699584 | tf_op jit(solution)/shard_map/rpm,mcq->rpcq/dot_general | solution.py:48
  217.2 0.0 copy-start.1
  217.2 2.0 copy-done.1
  219.2 0.1 slice_bitcast_fusion
  219.3 0.6 copy.22
  219.9 0.8 gather_fusion.1
  220.7 2.7 select_select_fusion
  223.4 1.4 bitcast_dynamic-update-slice_fusion
  224.8 2.0 select_select_fusion.4
  226.9 0.0 all-reduce.9.cloned.1.call-update
  226.9 0.2 all-reduce.11.cloned.1.call-start
  227.1 0.3 all-reduce.11.cloned.1.call-update
  227.5 1.0 slice_bitcast_fusion.2
  228.4 0.8 fusion.7
  229.3 68.1 %all-reduce.9.cloned.1.call-done = f32[4,128,128]{2,1,0:T(8,128)} async-done(((f32[4,128,128]{2,1,0:T(8,128)}), f32[4,128,128]{2,1,0:T(8,128)}) %all-reduce.9.cloned.1.call-update) | async-done | bytes 262160 | tf_op jit(solution)/shard_map/psum | solution.py:11
  297.4 118.7 %all-reduce.11.cloned.1.call-done = f32[128,16,128]{2,0,1:T(8,128)} async-done(((f32[128,16,128]{2,0,1:T(8,128)}), f32[128,16,128]{2,0,1:T(8,128)}) %all-reduce.11.cloned.1.call-update) | async-done | bytes 1048592 | tf_op jit(solution)/shard_map/psum | solution.py:11
  416.1 6.4 %subtract_bitcast_fusion = f32[4,1,128,16,1,128]{5,2,0,3,4,1:T(8,128)S(1)} fusion(f32[4,128,16,128]{3,1,0,2:T(8,128)} %fusion.7, f32[4,16]{0,1:T(8,128)S(1)} %copy.15, f32[128,16,128]{2,0,1:T(8,128)} %all-reduce.11.cloned.1.call-done, f32[4,128,128]{2,1,0:T(8,128)} %all-reduce.9.cloned.1.call-done), kind=kOutput, calls=%fused_computation.4 | convolution fusion | flops 1612709888 | bytes 9699584 | tf_op jit(solution)/shard_map/rpm,mcq->rpcq/dot_general | solution.py:48
  422.5 6.3 %copy.26 = f32[4,1,128,16,1,128]{5,4,3,2,1,0:T(1,128)} copy(f32[4,1,128,16,1,128]{5,2,0,3,4,1:T(8,128)S(1)} %subtract_bitcast_fusion) | data formatting | bytes 8388608 | tf_op jit(solution)/shard_map/broadcast_in_dim | solution.py:55
  (7 shorter events, 0.1 us)
Async XLA Ops:
  6.5 85.4 %all-reduce.5.cloned.1.call-start = ((), (), s32[]{:S(2)}) async-start(), calls=%async_computation | async-start | bytes 524288 | tf_op jit(solution)/shard_map/psum | solution.py:11
  11.2 2.0 copy-start
  13.2 0.7 copy-start.3
  14.0 4.9 %copy-start.2 = (f32[2,128,128]{2,1,0:T(8,128)S(1)}, f32[2,128,128]{2,1,0:T(8,128)}, u32[]{:S(2)}) copy-start(f32[2,128,128]{2,1,0:T(8,128)} %param.16) | copy-start | bytes 393220
  21.0 189.8 %all-reduce.7.cloned.1.call-start = ((), (), s32[]{:S(2)}) async-start(), calls=%async_computation.1 | async-start | bytes 2097152 | tf_op jit(solution)/shard_map/psum | solution.py:11
  21.7 275.7 %all-reduce.9.cloned.1.call-start = ((), (), s32[]{:S(2)}) async-start(), calls=%async_computation.2 | async-start | bytes 524288 | tf_op jit(solution)/shard_map/psum | solution.py:11
  217.2 2.0 copy-start.1
  226.9 189.2 %all-reduce.11.cloned.1.call-start = ((), (), s32[]{:S(2)}) async-start(), calls=%async_computation.3 | async-start | bytes 2097152 | tf_op jit(solution)/shard_map/psum | solution.py:11
Sparse Core Ops, SparseCore 0:
  21.1 70.7 all-reduce.4
  95.5 115.2 all-reduce.6
  227.0 70.3 all-reduce.8
  300.8 115.2 all-reduce.10
where the time goes:
time: 439 us; the launch traced here: 435 us
  waiting for transfers between devices  375 us (85%)
  matrix products  16.8 us (4%)
  local copies, waits for them, and re-layouts  15.3 us (3%)
  other arithmetic  14.6 us (3%)
  between operations  13.3 us (3%)
    psum x4, waiting for transfers between devices, spread(): return lax.psum(jnp.where(mine, shard, jnp.zeros_like(shard)), axis)  374 us
    dot_general x2, matrix products, trailing(): update = jnp.einsum('rpm,mcq->rpcq', l_panel, u_panel, precision=HIGH)  12.8 us
  transfers between devices with their start and end apart: 4, of which 4 were waited for; matrix products, arithmetic and copies ran while one was open for 1% of the time, Pallas kernels for 0%

commit v1 on v0

v1 whole, which is shorter than its diff:
```python
import jax
import jax.numpy as jnp
from jax import lax
from jax.experimental import pallas as pl
from jax.experimental.pallas import tpu as pltpu
from jax.sharding import PartitionSpec as P

HIGH = lax.Precision.HIGHEST
F32 = jnp.float32
BF16 = jnp.bfloat16
B = 128
RB = 4
CB = 16
NX = 4
NY = 4
NZ = 8
PANEL = CB * B + 256
TREE = PANEL // 4
LBLK = B + 16
LHALF = 2 * LBLK
N = 9
NL = 9
LAG = 2
R = TREE // N
RL = LHALF // NL


def split(x):
    hi = x.astype(BF16)
    return hi, (x - hi.astype(F32)).astype(BF16)


def dot3(a, b):
    mm = lambda u, v: jnp.dot(u, v, preferred_element_type=F32)
    return mm(a[0], b[0]) + (mm(a[0], b[1]) + mm(a[1], b[0]))


def high(a, b, dims=((1,), (0,))):
    return lax.dot_general(a, b, (dims, ((), ())), precision=HIGH, preferred_element_type=F32)


def kernel(values, fill, inverses, pivots, out, vals, u, lp, gmat, pmat, left, load_sem, out_sem,
           urecv, usib, usend, lrecv, lsend, esend, erecv):
    row = lax.axis_index("row")
    z = lax.axis_index("col")
    core = row % 2
    x = (row // 2) % NX
    y = row // (2 * NX)
    other = 1 - core
    e_src = 1 - core

    def at(x_, y_, core_, z_):
        return {"row": (y_ * NX + x_) * 2 + core_, "col": z_}

    xp, xm = (x + 1) % NX, (x + NX - 1) % NX
    yp, ym = (y + 1) % NY, (y + NY - 1) % NY
    zp, zm = (z + 1) % NZ, (z + NZ - 1) % NZ
    sibling = at(x, y, other, z)
    near = [at(xp, y, core, z), at(xm, y, core, z), at(x, yp, core, z), at(x, ym, core, z),
            at(x, y, core, zp), at(x, y, core, zm), sibling]
    is_root = row < 2

    def load(r, c):
        return pltpu.make_async_copy(values.at[r, :, c, 0, :], vals.at[r, c], load_sem.at[r, c])

    @pl.loop(0, CB)
    def _(c):
        load(0, c).start()

    for r in range(1, RB):
        load(r, 0).start()

    barrier = pltpu.get_barrier_semaphore()
    for dev in near:
        pl.semaphore_signal(barrier, inc=1, device_id=dev)

    @pl.when(is_root & (z == e_src))
    def _():
        @pl.loop(1, NZ)
        def _(j):
            pl.semaphore_signal(barrier, inc=1, device_id=at(x, y, core, (z + j) % NZ))

    @pl.when(is_root & (z != e_src))
    def _():
        pl.semaphore_signal(barrier, inc=1, device_id=at(x, y, core, e_src))

    @pl.loop(1, CB)
    def _(c):
        for r in range(1, RB):
            load(r, c).start()

    for k in range(2):
        pt = (lax.broadcasted_iota(jnp.int32, (B, B), 0) == pivots[k:k + 1, :]).astype(F32)
        pmat[k] = pt
        gmat[k] = high(inverses[k], pt, ((1,), (1,)))

    @pl.loop(0, CB)
    def _(c):
        load(0, c).wait()

    for r in range(1, RB):
        load(r, 0).wait()

    @pl.when(is_root)
    def _():
        @pl.loop(0, CB)
        def _(c):
            f = fill[0, 0, c].astype(F32)
            u[core, pl.ds(c * B, B), :] = vals[0, c] * f
            u[core, pl.ds(CB * B + B + c * 8, 8), :] = jnp.zeros((8, B), F32) + f

    @pl.when(z < 2)
    def _():
        for r in range(RB):
            f = fill[r, 0, 0].astype(F32)
            lp[z, pl.ds(r * LBLK, B), :] = vals[r, 0] * f
            lp[z, pl.ds(r * LBLK + B, 16), :] = jnp.zeros((16, B), F32) + f

    pl.semaphore_wait(barrier, len(near) + jnp.where(is_root, jnp.where(z == e_src, NZ - 1, 1), 0))

    def extra(z_):
        return pltpu.make_async_remote_copy(
            src_ref=u.at[core, pl.ds(0, B)], dst_ref=u.at[core, pl.ds(CB * B, B)],
            send_sem=esend.at[z_], recv_sem=erecv, device_id=at(x, y, core, z_))

    @pl.when(is_root & (z == e_src))
    def _():
        @pl.loop(1, NZ)
        def _(j):
            extra((z + j) % NZ).start()

        u[core, pl.ds(CB * B, B), :] = u[core, pl.ds(0, B), :]

    def tree(a, b):
        hops = jnp.where(b == 0, a, jnp.where(a == 0, 4 + b, a + b))
        to_a = ((b == 0) & (a < 3)) | ((b > 0) & (a == 3))
        to_b = (a > 0) & (b < 3)
        return hops, to_a, to_b

    mx, my = (NX - x) % NX, (NY - y) % NY
    trees = []
    for a, b, dev_a, dev_b in ((x, y, near[0], near[2]), (mx, my, near[1], near[3]),
                               (y, x, near[2], near[0]), (my, mx, near[3], near[1])):
        trees.append((*tree(a, b), dev_a, dev_b))
    ways = [[((z - k + NZ) % NZ, near[4]), ((k - z + NZ) % NZ, near[5])] for k in range(2)]

    def chunk(d, i, kind, dev):
        rows = u.at[core, pl.ds(d * TREE + i * R, R)]
        recv = usib.at[d] if kind == 2 else urecv.at[d, i]
        return pltpu.make_async_remote_copy(
            src_ref=rows, dst_ref=rows, send_sem=usend.at[d, kind], recv_sem=recv, device_id=dev)

    def lchunk(k, s, i, dev):
        rows = lp.at[k, pl.ds(s * LHALF + i * RL, RL)]
        return pltpu.make_async_remote_copy(
            src_ref=rows, dst_ref=rows, send_sem=lsend.at[k, s], recv_sem=lrecv.at[k, s, i], device_id=dev)

    @pl.loop(0, LAG * 7 + max(N, NL))
    def _(t):
        for d, (hops, to_a, to_b, dev_a, dev_b) in enumerate(trees):
            i = t - LAG * hops

            @pl.when((i >= 0) & (i < N))
            def _():
                @pl.when(hops > 0)
                def _():
                    chunk(d, i, 0, dev_a).wait_recv()

                if d == 3:
                    @pl.when(is_root & (z != e_src) & (i == (CB * B - 3 * TREE) // R))
                    def _():
                        extra(z).wait_recv()

                @pl.when(to_a)
                def _():
                    chunk(d, i, 0, dev_a).start()

                @pl.when(to_b)
                def _():
                    chunk(d, i, 1, dev_b).start()

                chunk(d, i, 2, sibling).start()

        for k in range(2):
            for s in range(2):
                hops, dev = ways[k][s]
                j = t - LAG * hops

                @pl.when((j >= 0) & (j < NL))
                def _():
                    @pl.when(hops > 0)
                    def _():
                        lchunk(k, s, j, dev).wait_recv()

                    @pl.when(hops < NZ - 1)
                    def _():
                        lchunk(k, s, j, dev).start()

    def whole(d, kind, panel):
        rows = u.at[panel, pl.ds(d * TREE, TREE)]
        return pltpu.make_async_remote_copy(
            src_ref=rows, dst_ref=rows, send_sem=usend.at[d, kind], recv_sem=usib.at[d], device_id=sibling)

    for d in range(4):
        whole(d, 2, other).wait_recv()

    panel = lambda k: jnp.concatenate([lp[k, pl.ds(r * LBLK, B), :] for r in range(RB)], axis=0)
    l_first = high(panel(0), gmat[0])
    u_01 = u[0, pl.ds(CB * B, B), :]
    f_col = jnp.concatenate(
        [jnp.broadcast_to(lp[1, pl.ds(r * LBLK + B, 1), :], (B, B)) for r in range(RB)], axis=0)
    second = panel(1) - f_col * high(l_first, u_01)
    l_second = high(second, gmat[1])
    q10 = split(high(u[1, pl.ds(CB * B, B), :], gmat[0]))
    left[:, 0:B] = l_first
    left[:, B:2 * B] = l_second

    @pl.loop(1, CB)
    def _(c):
        for r in range(1, RB):
            load(r, c).wait()

    @pl.when(is_root)
    def _():
        left[pl.ds(0, B), B:2 * B] = jnp.zeros((B, B), F32)
        own = pmat[core].T

        @pl.loop(0, CB)
        def _(c):
            vals[0, c] = high(own, vals[0, c])

    @pl.when(row == 0)
    def _():
        left[pl.ds(0, B), 0:B] = jnp.zeros((B, B), F32)

    @pl.when(row == 1)
    def _():
        left[pl.ds(0, B), 0:B] = high(pmat[1].T, left[pl.ds(0, B), 0:B])

    lhs = split(left[...])

    def store(r, c):
        return pltpu.make_async_copy(vals.at[r, c], out.at[r, :, c, 0, :], out_sem.at[r, c])

    @pl.loop(0, CB // 2)
    def _(j):
        c = 2 * j
        pair = lambda k: jnp.concatenate(
            [u[k, pl.ds(pl.multiple_of(c * B, B), B), :],
             u[k, pl.ds(pl.multiple_of(c * B + B, B), B), :]], axis=1)
        top = pair(0)
        top2 = split(top)
        f_row = jnp.concatenate([u[1, pl.ds(CB * B + B + c * 8, 1), :],
                                 u[1, pl.ds(CB * B + B + c * 8 + 8, 1), :]], axis=1)
        low2 = split(pair(1) - f_row * dot3(q10, top2))
        rhs = tuple(jnp.concatenate([a, b], axis=0) for a, b in zip(top2, low2))
        update = dot3(lhs, rhs)
        for r in range(RB):
            for e in range(2):
                f = fill[r, 0, c + e].astype(F32)
                vals[r, c + e] = (vals[r, c + e] - update[r * B:(r + 1) * B, e * B:(e + 1) * B]) * f

        @pl.when((j == 0) & (z < 2))
        def _():
            keep = jnp.where(z == 0, panel(0), second)
            done = high(keep, jnp.where(z == 0, inverses[0], inverses[1]))
            for r in range(RB):
                if r == 0:
                    @pl.when(row > z)
                    def _():
                        vals[0, 0] = done[0:B]
                else:
                    vals[r, 0] = done[r * B:(r + 1) * B]

        for r in range(RB):
            for e in range(2):
                store(r, c + e).start()

    for d, (hops, to_a, to_b, dev_a, dev_b) in enumerate(trees):
        @pl.when(to_a)
        def _():
            whole(d, 0, core).wait_send()

        @pl.when(to_b)
        def _():
            whole(d, 1, core).wait_send()

        whole(d, 2, core).wait_send()

    for k in range(2):
        for s in range(2):
            hops, dev = ways[k][s]

            @pl.when(hops < NZ - 1)
            def _():
                rows = lp.at[k, pl.ds(s * LHALF, LHALF)]
                pltpu.make_async_remote_copy(
                    src_ref=rows, dst_ref=rows, send_sem=lsend.at[k, s], recv_sem=lrecv.at[k, s, 0],
                    device_id=dev).wait_send()

    @pl.when(is_root & (z == e_src))
    def _():
        @pl.loop(1, NZ)
        def _(j):
            extra((z + j) % NZ).wait_send()

    @pl.loop(0, CB)
    def _(c):
        for r in range(RB):
            store(r, c).wait()


def per_device(values, fill, inverses, pivots):
    shape = (RB, B, CB, 1, B)
    vmem = pl.BlockSpec(memory_space=pltpu.VMEM)
    result = pl.pallas_call(
        kernel,
        out_shape=jax.ShapeDtypeStruct(shape, F32),
        in_specs=[pl.BlockSpec(memory_space=pltpu.HBM), pl.BlockSpec(memory_space=pltpu.SMEM), vmem, vmem],
        out_specs=pl.BlockSpec(memory_space=pl.ANY),
        scratch_shapes=[
            pltpu.VMEM((RB, CB, B, B), F32),
            pltpu.VMEM((2, PANEL, B), F32),
            pltpu.VMEM((2, RB * LBLK, B), F32),
            pltpu.VMEM((2, B, B), F32),
            pltpu.VMEM((2, B, B), F32),
            pltpu.VMEM((RB * B, 2 * B), F32),
            pltpu.SemaphoreType.DMA((RB, CB)),
            pltpu.SemaphoreType.DMA((RB, CB)),
            pltpu.SemaphoreType.DMA((4, N)),
            pltpu.SemaphoreType.DMA((4,)),
            pltpu.SemaphoreType.DMA((4, 3)),
            pltpu.SemaphoreType.DMA((2, 2, NL)),
            pltpu.SemaphoreType.DMA((2, 2)),
            pltpu.SemaphoreType.DMA((NZ,)),
            pltpu.SemaphoreType.DMA(()),
        ],
        compiler_params=pltpu.CompilerParams(
            collective_id=0, has_side_effects=True, vmem_limit_bytes=24 << 20),
    )(values.reshape(shape), fill.reshape(RB, 1, CB), inverses, pivots)
    return result.reshape(values.shape)


def solution(mesh):
    placed = (P(None, "row", None, None, "col", None), P(None, "row", None, "col"), P(), P())
    return jax.shard_map(
        per_device,
        mesh=mesh,
        in_specs=placed,
        out_specs=P(None, "row", None, None, "col", None),
        check_vma=False,
    )
```

time: 439 us -> 65.2 us (0.15)
  the two profiles are of different devices: /device:TPU:13 before, /device:TPU:32 now
where the time goes in v1:
time: 65.2 us; the launch traced here: 65 us
  Pallas kernels  58.6 us (90%)
  local copies, waits for them, and re-layouts  6.47 us (10%)
    pallas_call x1, Pallas kernels, per_device(): pl.pallas_call(kernel, out_shape=jax.ShapeDtypeStruct(shape, F32), in_spe...  58.6 us
    unnamed x9, local copies, waits for them, and re-layouts  6.47 us

profile of v1, /device:TPU:32, one launch (start us, length us, event | category | flops | bytes accessed | tf_op | source)
XLA Modules:
  0.0 65.0 jit_solution(18389003941015739327)
XLA Ops:
  0.0 0.0 copy-start
  0.0 2.2 %copy-done = f32[4,1,128,16,1,128]{5,4,3,2,1,0:T(1,128)S(1)} copy-done((f32[4,1,128,16,1,128]{5,4,3,2,1,0:T(1,128)S(1)}, f32[4,1,128,16,1,128]{5,4,3,2,1,0:T(1,128)}, u32[]{:S(2)}) %copy-start) | copy-done | bytes 4194328
  2.2 0.0 copy-start.1
  2.2 0.9 %copy-done.1 = f32[2,128,128]{2,1,0:T(8,128)S(1)} copy-done((f32[2,128,128]{2,1,0:T(8,128)S(1)}, f32[2,128,128]{2,1,0:T(8,128)}, u32[]{:S(2)}) %copy-start.1) | copy-done | bytes 131096
  3.1 0.0 copy-start.2
  3.1 0.7 %copy-done.2 = s32[4,1,16,1]{2,3,1,0:T(1,128)S(1)} copy-done((s32[4,1,16,1]{2,3,1,0:T(1,128)S(1)}, s32[4,1,16,1]{2,3,1,0:T(1,128)}, u32[]{:S(2)}) %copy-start.2) | copy-done | bytes 280
  3.8 0.0 copy-start.3
  3.8 0.7 %copy-done.3 = s32[2,128]{1,0:T(2,128)S(1)} copy-done((s32[2,128]{1,0:T(2,128)S(1)}, s32[2,128]{1,0:T(2,128)}, u32[]{:S(2)}) %copy-start.3) | copy-done | bytes 1048
  4.5 58.6 %shard_map.46 = f32[4,128,16,1,128]{4,3,2,1,0:T(1,128)S(1)} custom-call(f32[4,128,16,1,128]{4,3,2,1,0:T(1,128)S(1)} %bitcast.8, s32[4,1,16]{2,1,0:T(1,128)S(1)} %bitcast.9, f32[2,128,128]{2,1,0:T(8,128)S(1)} %copy-done.1, s32[2,128]{1,0:T(2,128)S(1)} %copy-done.3), custom_call_target="tpu_custom_call" | custom-call | tf_op jit(solution)/shard_map/pallas_call | solution.py:316
  63.0 2.0 %copy.8 = f32[4,1,128,16,1,128]{5,4,3,2,1,0:T(1,128)} copy(f32[4,1,128,16,1,128]{5,4,3,2,1,0:T(1,128)S(1)} %bitcast.7) | data formatting | bytes 8388608
Async XLA Ops:
  0.0 2.2 %copy-start = (f32[4,1,128,16,1,128]{5,4,3,2,1,0:T(1,128)S(1)}, f32[4,1,128,16,1,128]{5,4,3,2,1,0:T(1,128)}, u32[]{:S(2)}) copy-start(f32[4,1,128,16,1,128]{5,4,3,2,1,0:T(1,128)} %param.4) | copy-start | bytes 12582916
  2.2 0.9 %copy-start.1 = (f32[2,128,128]{2,1,0:T(8,128)S(1)}, f32[2,128,128]{2,1,0:T(8,128)}, u32[]{:S(2)}) copy-start(f32[2,128,128]{2,1,0:T(8,128)} %inverses.1) | copy-start | bytes 393220
  3.1 0.7 %copy-start.2 = (s32[4,1,16,1]{2,3,1,0:T(1,128)S(1)}, s32[4,1,16,1]{2,3,1,0:T(1,128)}, u32[]{:S(2)}) copy-start(s32[4,1,16,1]{2,3,1,0:T(1,128)} %param.5) | copy-start | bytes 772
  3.8 0.7 %copy-start.3 = (s32[2,128]{1,0:T(2,128)S(1)}, s32[2,128]{1,0:T(2,128)}, u32[]{:S(2)}) copy-start(s32[2,128]{1,0:T(2,128)} %pivots.1) | copy-start | bytes 3076

commit v2 on v1

v2 whole, which is shorter than its diff:
```python
import jax
import jax.numpy as jnp
from jax import lax
from jax.experimental import pallas as pl
from jax.experimental.pallas import tpu as pltpu
from jax.sharding import PartitionSpec as P

HIGH = lax.Precision.HIGHEST
F32 = jnp.float32
BF16 = jnp.bfloat16
B = 128
RB = 4
CB = 16
NX = 4
NY = 4
NZ = 8
EXTRA = CB * B
ER = 40
PANEL = EXTRA + 4 * ER
N = 8
R = CB * B // 4 // N
NL = 8
RL = RB * B // NL
LAG = 7


def split(x):
    hi = x.astype(BF16)
    return hi, (x - hi.astype(F32)).astype(BF16)


def dot3(a, b):
    mm = lambda u, v: jnp.dot(u, v, preferred_element_type=F32)
    return mm(a[0], b[0]) + (mm(a[0], b[1]) + mm(a[1], b[0]))


def high(a, b, dims=((1,), (0,))):
    return lax.dot_general(a, b, (dims, ((), ())), precision=HIGH, preferred_element_type=F32)


def kernel(values, fill_hbm, inverses_hbm, pivots_hbm, out, vals, u, lp, fcol, gmat, pmat, left, fill, inverses,
           pivots, load_sem, out_sem, small_sem, urecv, usib, usend, lrecv, lsend, frecv, fsend, esend, erecv):
    row = lax.axis_index("row")
    z = lax.axis_index("col")
    core = row % 2
    x = (row // 2) % NX
    y = row // (2 * NX)
    other = 1 - core
    e_src = 1 - core

    def at(x_, y_, core_, z_):
        return {"row": (y_ * NX + x_) * 2 + core_, "col": z_}

    zp, zm = (z + 1) % NZ, (z + NZ - 1) % NZ
    sibling = at(x, y, other, z)
    cube = [at(x + 1 - 2 * (x % 2), y, core, z), at(3 - x, y, core, z),
            at(x, y + 1 - 2 * (y % 2), core, z), at(x, 3 - y, core, z)]
    bits = [(x + 1) // 2 % 2, x // 2, (y + 1) // 2 % 2, y // 2]
    near = cube + [at(x, y, core, zp), at(x, y, core, zm), sibling]
    is_root = row < 2

    def load(r, c):
        return pltpu.make_async_copy(values.at[r, :, c, 0, :], vals.at[r, c], load_sem.at[r, c])

    small = [pltpu.make_async_copy(fill_hbm, fill, small_sem.at[0]),
             pltpu.make_async_copy(pivots_hbm, pivots, small_sem.at[1]),
             pltpu.make_async_copy(inverses_hbm, inverses, small_sem.at[2])]
    for copy in small:
        copy.start()

    @pl.loop(0, CB)
    def _(c):
        load(0, c).start()

    for r in range(1, RB):
        load(r, 0).start()

    barrier = pltpu.get_barrier_semaphore()
    for dev in near:
        pl.semaphore_signal(barrier, inc=1, device_id=dev)

    @pl.when(is_root & (z == e_src))
    def _():
        @pl.loop(1, NZ)
        def _(j):
            pl.semaphore_signal(barrier, inc=1, device_id=at(x, y, core, (z + j) % NZ))

    @pl.when(is_root & (z != e_src))
    def _():
        pl.semaphore_signal(barrier, inc=1, device_id=at(x, y, core, e_src))

    @pl.loop(1, CB)
    def _(c):
        for r in range(1, RB):
            load(r, c).start()

    for copy in small:
        copy.wait()

    for k in range(2):
        pt = (lax.broadcasted_iota(jnp.int32, (B, B), 0) == pivots[k:k + 1, :]).astype(F32)
        pmat[k] = pt
        gmat[k] = high(inverses[k], pt, ((1,), (1,)))

    load(0, 0).wait()

    @pl.when(is_root)
    def _():
        u[core, 0:B, :] = vals[0, 0] * fill[0, 0, 0].astype(F32)

    pl.semaphore_wait(barrier, len(near) + jnp.where(is_root, jnp.where(z == e_src, NZ - 1, 1), 0))

    def extra(z_):
        return pltpu.make_async_remote_copy(
            src_ref=u.at[core, pl.ds(0, B)], dst_ref=u.at[core, pl.ds(EXTRA, B)],
            send_sem=esend.at[z_], recv_sem=erecv, device_id=at(x, y, core, z_))

    @pl.when(is_root & (z == e_src))
    def _():
        @pl.loop(1, NZ)
        def _(j):
            extra((z + j) % NZ).start()

        u[core, pl.ds(EXTRA, B), :] = u[core, pl.ds(0, B), :]

    @pl.loop(1, CB)
    def _(c):
        load(0, c).wait()

    for r in range(1, RB):
        load(r, 0).wait()

    @pl.when(is_root)
    def _():
        @pl.loop(0, CB)
        def _(c):
            f = fill[0, 0, c].astype(F32)

            @pl.when(c > 0)
            def _():
                u[core, pl.ds(c * B, B), :] = vals[0, c] * f

            u[core, pl.ds(EXTRA + B + c, 1), :] = jnp.zeros((1, B), F32) + f

        u[core, pl.ds(EXTRA + B + CB, CB), :] = jnp.zeros((CB, B), F32)

    @pl.when(z < 2)
    def _():
        for r in range(RB):
            f = fill[r, 0, 0].astype(F32)
            lp[z, pl.ds(r * B, B), :] = vals[r, 0] * f

            @pl.when(z == 1)
            def _():
                fcol[pl.ds(r, 1), :] = jnp.zeros((1, B), F32) + f

    @pl.when(z == 1)
    def _():
        fcol[pl.ds(RB, RB), :] = jnp.zeros((RB, B), F32)

    weight = bits[0] + bits[1] + bits[2] + bits[3]
    top = weight == 0
    trees = []
    for d in range(4):
        rel = [bits[(d + q) % 4] if q < 4 else 1 - bits[d] for q in range(1, 5)]
        last = jnp.where(rel[3] == 1, 4, jnp.where(rel[2] == 1, 3, jnp.where(rel[1] == 1, 2, rel[0])))
        hops = jnp.where(top, 0, 1 + rel[0] + rel[1] + rel[2] + rel[3])
        kids = [((d + q) % 4, last < q) for q in range(1, 4)]
        kids.append((d, top | ((last >= 1) & (last <= 3))))
        trees.append((hops, kids))

    def chunk(d, i, kind, dev):
        rows = u.at[core, pl.ds((4 * (i // 2) + d) * B + i % 2 * R, R)]
        recv = usib.at[d] if kind == 4 else urecv.at[d, i]
        return pltpu.make_async_remote_copy(
            src_ref=rows, dst_ref=rows, send_sem=usend.at[d, kind], recv_sem=recv, device_id=dev)

    def echunk(d, kind, dev):
        rows = u.at[core, pl.ds(EXTRA + d * ER, ER)]
        recv = usib.at[d] if kind == 4 else urecv.at[d, N]
        return pltpu.make_async_remote_copy(
            src_ref=rows, dst_ref=rows, send_sem=usend.at[d, kind], recv_sem=recv, device_id=dev)

    ways = []
    for k in range(2):
        for s in range(2):
            hops = (z - k + NZ) % NZ if s == 0 else (k - z + NZ) % NZ
            count = lambda h: jnp.where(h <= 3, NL, jnp.where(h == 4, NL // 2, 0))
            ways.append((k, s, hops, count(hops), count(hops + 1), near[4 + s]))

    def lchunk(k, s, j, dev):
        rows = lp.at[k, pl.ds((j + s * (NL // 2)) % NL * RL, RL)]
        return pltpu.make_async_remote_copy(
            src_ref=rows, dst_ref=rows, send_sem=lsend.at[k, s], recv_sem=lrecv.at[k, s, j], device_id=dev)

    def fcopy(s):
        return pltpu.make_async_remote_copy(
            src_ref=fcol, dst_ref=fcol, send_sem=fsend.at[s], recv_sem=frecv, device_id=near[4 + s])

    f_up = (z - 1 + NZ) % NZ
    f_to = [f_up <= 3, (f_up == 0) | ((f_up >= 6))]

    @pl.loop(0, LAG * 5 + N + 1)
    def _(t):
        for k, s, hops, get, give, dev in ways:
            j = t - LAG * hops

            @pl.when((j >= 0) & (j < get))
            def _():
                @pl.when(hops > 0)
                def _():
                    lchunk(k, s, j, dev).wait_recv()

                @pl.when(j < give)
                def _():
                    lchunk(k, s, j, dev).start()

        for d, (hops, kids) in enumerate(trees):
            i = t - LAG * hops

            @pl.when((i >= 0) & (i < N))
            def _():
                @pl.when(hops > 0)
                def _():
                    chunk(d, i, d, sibling).wait_recv()

                for m, (bit, has) in enumerate(kids):
                    @pl.when(has)
                    def _():
                        chunk(d, i, m, cube[bit]).start()

                chunk(d, i, 4, sibling).start()

            @pl.when(i == N)
            def _():
                @pl.when(hops > 0)
                def _():
                    echunk(d, d, sibling).wait_recv()

                if d == 0:
                    @pl.when(is_root & (z != e_src))
                    def _():
                        extra(z).wait_recv()

                for m, (bit, has) in enumerate(kids):
                    @pl.when(has)
                    def _():
                        echunk(d, m, cube[bit]).start()

                echunk(d, 4, sibling).start()

        @pl.when(t == LAG * jnp.where(f_up <= 4, f_up, NZ - f_up))
        def _():
            @pl.when(f_up > 0)
            def _():
                fcopy(0).wait_recv()

            for s in range(2):
                @pl.when(f_to[s])
                def _():
                    fcopy(s).start()

    def whole(d, kind, panel):
        rows = u.at[panel, pl.ds(d * (CB * B // 4), CB * B // 4 + ER)]
        return pltpu.make_async_remote_copy(
            src_ref=rows, dst_ref=rows, send_sem=usend.at[d, kind], recv_sem=usib.at[d], device_id=sibling)

    for d in range(4):
        whole(d, 4, other).wait_recv()

    panel = lambda k: lp[k]
    l_first = high(panel(0), gmat[0])
    u_01 = u[0, pl.ds(EXTRA, B), :]
    f_col = jnp.concatenate(
        [jnp.broadcast_to(fcol[pl.ds(r, 1), :], (B, B)) for r in range(RB)], axis=0)
    second = panel(1) - f_col * high(l_first, u_01)
    l_second = high(second, gmat[1])
    q10 = split(high(u[1, pl.ds(EXTRA, B), :], gmat[0]))
    left[:, 0:B] = l_first
    left[:, B:2 * B] = l_second

    @pl.loop(1, CB)
    def _(c):
        for r in range(1, RB):
            load(r, c).wait()

    @pl.when(is_root)
    def _():
        left[pl.ds(0, B), B:2 * B] = jnp.zeros((B, B), F32)
        own = pmat[core].T

        @pl.loop(0, CB)
        def _(c):
            vals[0, c] = high(own, vals[0, c])

    @pl.when(row == 0)
    def _():
        left[pl.ds(0, B), 0:B] = jnp.zeros((B, B), F32)

    @pl.when(row == 1)
    def _():
        left[pl.ds(0, B), 0:B] = high(pmat[1].T, left[pl.ds(0, B), 0:B])

    lhs = split(left[...])

    def store(r, c):
        return pltpu.make_async_copy(vals.at[r, c], out.at[r, :, c, 0, :], out_sem.at[r, c])

    @pl.loop(0, CB // 2)
    def _(j):
        c = 2 * j
        pair = lambda k: jnp.concatenate(
            [u[k, pl.ds(pl.multiple_of(c * B, B), B), :],
             u[k, pl.ds(pl.multiple_of(c * B + B, B), B), :]], axis=1)
        top = pair(0)
        top2 = split(top)
        f_row = jnp.concatenate([u[1, pl.ds(EXTRA + B + c, 1), :],
                                 u[1, pl.ds(EXTRA + B + c + 1, 1), :]], axis=1)
        low2 = split(pair(1) - f_row * dot3(q10, top2))
        rhs = tuple(jnp.concatenate([a, b], axis=0) for a, b in zip(top2, low2))
        update = dot3(lhs, rhs)
        for r in range(RB):
            for e in range(2):
                f = fill[r, 0, c + e].astype(F32)
                vals[r, c + e] = (vals[r, c + e] - update[r * B:(r + 1) * B, e * B:(e + 1) * B]) * f

        @pl.when((j == 0) & (z < 2))
        def _():
            keep = jnp.where(z == 0, panel(0), second)
            done = high(keep, jnp.where(z == 0, inverses[0], inverses[1]))
            for r in range(RB):
                if r == 0:
                    @pl.when(row > z)
                    def _():
                        vals[0, 0] = done[0:B]
                else:
                    vals[r, 0] = done[r * B:(r + 1) * B]

        for r in range(RB):
            for e in range(2):
                store(r, c + e).start()

    for d, (hops, kids) in enumerate(trees):
        for m, (bit, has) in enumerate(kids):
            @pl.when(has)
            def _():
                whole(d, m, core).wait_send()

        whole(d, 4, core).wait_send()

    for k, s, hops, get, give, dev in ways:
        for amount in (NL // 2, NL):
            @pl.when(give == amount)
            def _():
                rows = lp.at[k, pl.ds(0, amount * RL)]
                pltpu.make_async_remote_copy(
                    src_ref=rows, dst_ref=rows, send_sem=lsend.at[k, s], recv_sem=lrecv.at[k, s, 0],
                    device_id=dev).wait_send()

    for s in range(2):
        @pl.when(f_to[s])
        def _():
            fcopy(s).wait_send()

    @pl.when(is_root & (z == e_src))
    def _():
        @pl.loop(1, NZ)
        def _(j):
            extra((z + j) % NZ).wait_send()

    @pl.loop(0, CB)
    def _(c):
        for r in range(RB):
            store(r, c).wait()


def per_device(values, fill, inverses, pivots):
    shape = (RB, B, CB, 1, B)
    hbm = lambda a: pltpu.with_memory_space_constraint(a, pltpu.HBM)
    result = pl.pallas_call(
        kernel,
        out_shape=jax.ShapeDtypeStruct(shape, F32),
        in_specs=[pl.BlockSpec(memory_space=pltpu.HBM)] * 4,
        out_specs=pl.BlockSpec(memory_space=pl.ANY),
        scratch_shapes=[
            pltpu.VMEM((RB, CB, B, B), F32),
            pltpu.VMEM((2, PANEL, B), F32),
            pltpu.VMEM((2, RB * B, B), F32),
            pltpu.VMEM((2 * RB, B), F32),
            pltpu.VMEM((2, B, B), F32),
            pltpu.VMEM((2, B, B), F32),
            pltpu.VMEM((RB * B, 2 * B), F32),
            pltpu.SMEM((RB, 1, CB), jnp.int32),
            pltpu.VMEM((2, B, B), F32),
            pltpu.VMEM((2, B), jnp.int32),
            pltpu.SemaphoreType.DMA((RB, CB)),
            pltpu.SemaphoreType.DMA((RB, CB)),
            pltpu.SemaphoreType.DMA((3,)),
            pltpu.SemaphoreType.DMA((4, N + 1)),
            pltpu.SemaphoreType.DMA((4,)),
            pltpu.SemaphoreType.DMA((4, 5)),
            pltpu.SemaphoreType.DMA((2, 2, NL)),
            pltpu.SemaphoreType.DMA((2, 2)),
            pltpu.SemaphoreType.DMA(()),
            pltpu.SemaphoreType.DMA((2,)),
            pltpu.SemaphoreType.DMA((NZ,)),
            pltpu.SemaphoreType.DMA(()),
        ],
        compiler_params=pltpu.CompilerParams(
            collective_id=0, has_side_effects=True, vmem_limit_bytes=24 << 20),
    )(hbm(values.reshape(shape)), hbm(fill.reshape(RB, 1, CB)), hbm(inverses), hbm(pivots))
    return result.reshape(values.shape)


def solution(mesh):
    placed = (P(None, "row", None, None, "col", None), P(None, "row", None, "col"), P(), P())
    return jax.shard_map(
        per_device,
        mesh=mesh,
        in_specs=placed,
        out_specs=P(None, "row", None, None, "col", None),
        check_vma=False,
    )
```

time: 65.2 us -> 43.2 us (0.66)
  the two profiles are of different devices: /device:TPU:32 before, /device:TPU:13 now
where the time goes in v2:
time: 43.2 us
  Pallas kernels  41.1 us (95%)
  local copies, waits for them, and re-layouts  2.02 us (5%)
    pallas_call x1, Pallas kernels, per_device(): pl.pallas_call(kernel, out_shape=jax.ShapeDtypeStruct(shape, F32), in_spe...  41.1 us
    unnamed x1, local copies, waits for them, and re-layouts  2.02 us

profile of v2, /device:TPU:13, one launch (start us, length us, event | category | flops | bytes accessed | tf_op | source)
XLA Modules:
  0.0 43.2 jit_solution(15139775028686496152)
XLA Ops:
  0.0 41.1 %shard_map.46 = f32[4,128,16,1,128]{4,3,2,1,0:T(1,128)S(1)} custom-call(f32[4,128,16,1,128]{4,3,2,1,0:T(1,128)} %bitcast.8, s32[4,1,16]{2,1,0:T(1,128)} %bitcast.9, f32[2,128,128]{2,1,0:T(8,128)} %inverses_hbm.1, s32[2,128]{1,0:T(2,128)} %pivots_hbm.1), custom_call_target="tpu_custom_call" | custom-call | tf_op jit(solution)/shard_map/pallas_call | solution.py:380
  41.1 2.0 %copy.8 = f32[4,1,128,16,1,128]{5,4,3,2,1,0:T(1,128)} copy(f32[4,1,128,16,1,128]{5,4,3,2,1,0:T(1,128)S(1)} %bitcast.7) | data formatting | bytes 8388608

commit v3 on v2

--- a/solution.py
+++ b/solution.py
@@ -21,7 +21,9 @@
 R = CB * B // 4 // N
 NL = 8
 RL = RB * B // NL
-LAG = 7
+LA = 4
+LB = 2
+LROOT = 8
 
 
 def split(x):
@@ -39,7 +41,8 @@
 
 
 def kernel(values, fill_hbm, inverses_hbm, pivots_hbm, out, vals, u, lp, fcol, gmat, pmat, left, fill, inverses,
-           pivots, load_sem, out_sem, small_sem, urecv, usib, usend, lrecv, lsend, frecv, fsend, esend, erecv):
+           pivots, load_sem, out_sem, small_sem, urecv, usib, usend, lrecv, lsend, frecv, fsend, esend, erecv,
+           ready, eready):
     row = lax.axis_index("row")
     z = lax.axis_index("col")
     core = row % 2
@@ -56,38 +59,47 @@
     cube = [at(x + 1 - 2 * (x % 2), y, core, z), at(3 - x, y, core, z),
             at(x, y + 1 - 2 * (y % 2), core, z), at(x, 3 - y, core, z)]
     bits = [(x + 1) // 2 % 2, x // 2, (y + 1) // 2 % 2, y // 2]
-    near = cube + [at(x, y, core, zp), at(x, y, core, zm), sibling]
+    above, below = at(x, y, core, zp), at(x, y, core, zm)
+    near = [above, below]
     is_root = row < 2
 
     def load(r, c):
         return pltpu.make_async_copy(values.at[r, :, c, 0, :], vals.at[r, c], load_sem.at[r, c])
+
+    up, down = z <= 4, (z <= 1) | (z >= 5)
+    from_below, from_above = (z >= 1) & (z <= 5), (z == 0) | (z >= 4)
+    barrier = pltpu.get_barrier_semaphore()
+    for dev in cube + [sibling]:
+        pl.semaphore_signal(barrier, inc=1, device_id=dev)
+
+    @pl.when(up)
+    def _():
+        pl.semaphore_signal(barrier, inc=1, device_id=above)
+
+    @pl.when(down)
+    def _():
+        pl.semaphore_signal(barrier, inc=1, device_id=below)
+
+    @pl.when(is_root & (z == e_src))
+    def _():
+        @pl.loop(1, NZ)
+        def _(j):
+            pl.semaphore_signal(barrier, inc=1, device_id=at(x, y, core, (z + j) % NZ))
 
     small = [pltpu.make_async_copy(fill_hbm, fill, small_sem.at[0]),
              pltpu.make_async_copy(pivots_hbm, pivots, small_sem.at[1]),
              pltpu.make_async_copy(inverses_hbm, inverses, small_sem.at[2])]
-    for copy in small:
-        copy.start()
+    small[0].start()
 
     @pl.loop(0, CB)
-    def _(c):
-        load(0, c).start()
+    def _(n):
+        load(0, n % 4 * 4 + n // 4).start()
 
     for r in range(1, RB):
         load(r, 0).start()
 
-    barrier = pltpu.get_barrier_semaphore()
-    for dev in near:
-        pl.semaphore_signal(barrier, inc=1, device_id=dev)
-
-    @pl.when(is_root & (z == e_src))
-    def _():
-        @pl.loop(1, NZ)
-        def _(j):
-            pl.semaphore_signal(barrier, inc=1, device_id=at(x, y, core, (z + j) % NZ))
-
-    @pl.when(is_root & (z != e_src))
-    def _():
-        pl.semaphore_signal(barrier, inc=1, device_id=at(x, y, core, e_src))
+    for copy in small[1:]:
+        copy.start()
 
     @pl.loop(1, CB)
     def _(c):
@@ -97,57 +109,37 @@
     for copy in small:
         copy.wait()
 
-    for k in range(2):
-        pt = (lax.broadcasted_iota(jnp.int32, (B, B), 0) == pivots[k:k + 1, :]).astype(F32)
-        pmat[k] = pt
-        gmat[k] = high(inverses[k], pt, ((1,), (1,)))
-
-    load(0, 0).wait()
-
-    @pl.when(is_root)
-    def _():
-        u[core, 0:B, :] = vals[0, 0] * fill[0, 0, 0].astype(F32)
-
-    pl.semaphore_wait(barrier, len(near) + jnp.where(is_root, jnp.where(z == e_src, NZ - 1, 1), 0))
+    def inverse_products():
+        for k in range(2):
+            pt = (lax.broadcasted_iota(jnp.int32, (B, B), 0) == pivots[k:k + 1, :]).astype(F32)
+            pmat[k] = pt
+            gmat[k] = high(inverses[k], pt, ((1,), (1,)))
+
+    pl.semaphore_wait(barrier, 5 + jnp.where(from_below, 1, 0) + jnp.where(from_above, 1, 0)
+                      + jnp.where(is_root & (z != e_src), 1, 0))
+
+    @pl.when(from_below)
+    def _():
+        pl.semaphore_signal(ready.at[0], inc=1, device_id=below)
+
+    @pl.when(from_above)
+    def _():
+        pl.semaphore_signal(ready.at[1], inc=1, device_id=above)
+
+    @pl.when(is_root & (z != e_src))
+    def _():
+        pl.semaphore_signal(eready.at[z], inc=1, device_id=at(x, y, core, e_src))
 
     def extra(z_):
         return pltpu.make_async_remote_copy(
             src_ref=u.at[core, pl.ds(0, B)], dst_ref=u.at[core, pl.ds(EXTRA, B)],
             send_sem=esend.at[z_], recv_sem=erecv, device_id=at(x, y, core, z_))
 
-    @pl.when(is_root & (z == e_src))
-    def _():
-        @pl.loop(1, NZ)
-        def _(j):
-            extra((z + j) % NZ).start()
-
-        u[core, pl.ds(EXTRA, B), :] = u[core, pl.ds(0, B), :]
-
-    @pl.loop(1, CB)
-    def _(c):
-        load(0, c).wait()
-
-    for r in range(1, RB):
-        load(r, 0).wait()
-
-    @pl.when(is_root)
-    def _():
-        @pl.loop(0, CB)
-        def _(c):
-            f = fill[0, 0, c].astype(F32)
-
-            @pl.when(c > 0)
-            def _():
-                u[core, pl.ds(c * B, B), :] = vals[0, c] * f
-
-            u[core, pl.ds(EXTRA + B + c, 1), :] = jnp.zeros((1, B), F32) + f
-
-        u[core, pl.ds(EXTRA + B + CB, CB), :] = jnp.zeros((CB, B), F32)
-
     @pl.when(z < 2)
     def _():
         for r in range(RB):
             f = fill[r, 0, 0].astype(F32)
+            load(r, 0).wait()
             lp[z, pl.ds(r * B, B), :] = vals[r, 0] * f
 
             @pl.when(z == 1)
@@ -157,6 +149,19 @@
     @pl.when(z == 1)
     def _():
         fcol[pl.ds(RB, RB), :] = jnp.zeros((RB, B), F32)
+
+    @pl.when(z >= 2)
+    def _():
+        for r in range(RB):
+            load(r, 0).wait()
+
+    @pl.when(row >= 2)
+    def _():
+        @pl.loop(1, CB)
+        def _(c):
+            load(0, c).wait()
+
+        inverse_products()
 
     weight = bits[0] + bits[1] + bits[2] + bits[3]
     top = weight == 0
@@ -170,10 +175,15 @@
         trees.append((hops, kids))
 
     def chunk(d, i, kind, dev):
-        rows = u.at[core, pl.ds((4 * (i // 2) + d) * B + i % 2 * R, R)]
-        recv = usib.at[d] if kind == 4 else urecv.at[d, i]
+        rows = u.at[core, pl.ds(d * 4 * B + i * R, R)]
+        recv = urecv.at[d, i]
         return pltpu.make_async_remote_copy(
             src_ref=rows, dst_ref=rows, send_sem=usend.at[d, kind], recv_sem=recv, device_id=dev)
+
+    def to_sibling(d, i):
+        rows = u.at[core, pl.ds(d * 4 * B + (i - 3) * R, 4 * R)]
+        return pltpu.make_async_remote_copy(
+            src_ref=rows, dst_ref=rows, send_sem=usend.at[d, 4], recv_sem=usib.at[d], device_id=sibling)
 
     def echunk(d, kind, dev):
         rows = u.at[core, pl.ds(EXTRA + d * ER, ER)]
@@ -186,7 +196,7 @@
         for s in range(2):
             hops = (z - k + NZ) % NZ if s == 0 else (k - z + NZ) % NZ
             count = lambda h: jnp.where(h <= 3, NL, jnp.where(h == 4, NL // 2, 0))
-            ways.append((k, s, hops, count(hops), count(hops + 1), near[4 + s]))
+            ways.append((k, s, hops, count(hops), count(hops + 1), near[s]))
 
     def lchunk(k, s, j, dev):
         rows = lp.at[k, pl.ds((j + s * (NL // 2)) % NL * RL, RL)]
@@ -195,61 +205,25 @@
 
     def fcopy(s):
         return pltpu.make_async_remote_copy(
-            src_ref=fcol, dst_ref=fcol, send_sem=fsend.at[s], recv_sem=frecv, device_id=near[4 + s])
+            src_ref=fcol, dst_ref=fcol, send_sem=fsend.at[s], recv_sem=frecv, device_id=near[s])
 
     f_up = (z - 1 + NZ) % NZ
     f_to = [f_up <= 3, (f_up == 0) | ((f_up >= 6))]
 
-    @pl.loop(0, LAG * 5 + N + 1)
-    def _(t):
-        for k, s, hops, get, give, dev in ways:
-            j = t - LAG * hops
-
-            @pl.when((j >= 0) & (j < get))
-            def _():
-                @pl.when(hops > 0)
-                def _():
-                    lchunk(k, s, j, dev).wait_recv()
-
-                @pl.when(j < give)
-                def _():
-                    lchunk(k, s, j, dev).start()
-
-        for d, (hops, kids) in enumerate(trees):
-            i = t - LAG * hops
-
-            @pl.when((i >= 0) & (i < N))
-            def _():
-                @pl.when(hops > 0)
-                def _():
-                    chunk(d, i, d, sibling).wait_recv()
-
-                for m, (bit, has) in enumerate(kids):
-                    @pl.when(has)
-                    def _():
-                        chunk(d, i, m, cube[bit]).start()
-
-                chunk(d, i, 4, sibling).start()
-
-            @pl.when(i == N)
-            def _():
-                @pl.when(hops > 0)
-                def _():
-                    echunk(d, d, sibling).wait_recv()
-
-                if d == 0:
-                    @pl.when(is_root & (z != e_src))
-                    def _():
-                        extra(z).wait_recv()
-
-                for m, (bit, has) in enumerate(kids):
-                    @pl.when(has)
-                    def _():
-                        echunk(d, m, cube[bit]).start()
-
-                echunk(d, 4, sibling).start()
-
-        @pl.when(t == LAG * jnp.where(f_up <= 4, f_up, NZ - f_up))
+    early = [top | (bits[d] == 1) for d in range(4)]
+    first_up, first_down = jnp.where(z >= 1, z - 1, 0), jnp.where(z == 1, 0, (NZ - z) % NZ)
+    f_hops = jnp.where(f_up <= 4, f_up, NZ - f_up)
+
+    start = jnp.where(top, LROOT, LB)
+
+    def columns(n):
+        base = n - start + LA * weight
+        for s, (sends, least) in enumerate(((up, first_up), (down, first_down))):
+            @pl.when(sends & (base == LA * least))
+            def _():
+                pl.semaphore_wait(ready.at[s], 1)
+
+        @pl.when(base == LA * f_hops)
         def _():
             @pl.when(f_up > 0)
             def _():
@@ -260,38 +234,166 @@
                 def _():
                     fcopy(s).start()
 
+        for k, s, hops, get, give, dev in ways:
+            j = base - LA * hops
+
+            @pl.when((j >= 0) & (j < get))
+            def _():
+                @pl.when(hops > 0)
+                def _():
+                    lchunk(k, s, j, dev).wait_recv()
+
+                @pl.when(j < give)
+                def _():
+                    lchunk(k, s, j, dev).start()
+
+    def rows_of(d, i):
+        @pl.when(weight > 0)
+        def _():
+            chunk(d, i, d, sibling).wait_recv()
+
+        for m, (bit, has) in enumerate(trees[d][1]):
+            @pl.when(has)
+            def _():
+                chunk(d, i, m, cube[bit]).start()
+
+        @pl.when(i % 4 == 3)
+        def _():
+            to_sibling(d, i).start()
+
+    def extra_of(d):
+        @pl.when(weight > 0)
+        def _():
+            echunk(d, d, sibling).wait_recv()
+
+        for m, (bit, has) in enumerate(trees[d][1]):
+            @pl.when(has)
+            def _():
+                echunk(d, m, cube[bit]).start()
+
+        echunk(d, 4, sibling).start()
+
+    @pl.when(is_root)
+    def _():
+        for c in range(CB):
+            u[core, EXTRA + B + c:EXTRA + B + c + 1, :] = jnp.zeros((1, B), F32) + fill[0, 0, c].astype(F32)
+
+        u[core, EXTRA + B + CB:EXTRA + B + 2 * CB, :] = jnp.zeros((CB, B), F32)
+
+    @pl.loop(jnp.minimum(start - LA * weight, 0), 0)
+    def _(n):
+        columns(n)
+
+    @pl.loop(0, N)
+    def _(i):
+        @pl.when(is_root & (i % 2 == 0))
+        def _():
+            for d in range(4):
+                c = 4 * d + i // 2
+                if d == 0:
+                    @pl.when(i > 0)
+                    def _():
+                        load(0, c).wait()
+                else:
+                    load(0, c).wait()
+
+                u[core, pl.ds(c * B, B), :] = vals[0, c] * fill[0, 0, c].astype(F32)
+
+        for d in range(4):
+            @pl.when(early[d])
+            def _():
+                rows_of(d, i)
+
+        @pl.when(is_root & (z == e_src) & (i == 0))
+        def _():
+            u[core, pl.ds(EXTRA, B), :] = u[core, pl.ds(0, B), :]
+
+            pl.semaphore_wait(eready.at[1 - e_src], 1)
+            extra(1 - e_src).start()
+
+        @pl.when(is_root & (z == e_src) & (i == 3))
+        def _():
+            @pl.loop(2, NZ)
+            def _(j):
+                pl.semaphore_wait(eready.at[j], 1)
+                extra(j).start()
+
+        columns(i)
+
+    @pl.when(is_root & (z != e_src))
+    def _():
+        extra(z).wait_recv()
+
+    for d in range(4):
+        @pl.when(early[d])
+        def _():
+            extra_of(d)
+
+    @pl.when(is_root)
+    def _():
+        inverse_products()
+        pmat[core] = pmat[core].T
+
+    @pl.loop(N, jnp.maximum(LA * (4 - weight) + start + NL, N))
+    def _(n):
+        columns(n)
+
+        @pl.when(is_root & (n < N + CB))
+        def _():
+            own = pmat[core].astype(BF16)
+            v = vals[0, n - N]
+            first = v.astype(BF16)
+            rest = v - first.astype(F32)
+            second_ = rest.astype(BF16)
+            third = (rest - second_.astype(F32)).astype(BF16)
+            mm = lambda a: jnp.dot(own, a, preferred_element_type=F32)
+            vals[0, n - N] = mm(first) + (mm(second_) + mm(third))
+
+    panel = lambda k: lp[k]
+    for half in range(2):
+        if half == 1:
+            g_first, g_second = split(gmat[0]), split(gmat[1])
+            l_first = dot3(split(panel(0)), g_first)
+            left[:, 0:B] = l_first
+
+        for d in range(4):
+            @pl.when(~early[d])
+            def _():
+                @pl.loop(4 * half, 4 * half + 4)
+                def _(i):
+                    chunk(d, i, d, sibling).wait_recv()
+
+                to_sibling(d, 4 * half + 3).start()
+
+    for d in range(4):
+        @pl.when(~early[d])
+        def _():
+            echunk(d, d, sibling).wait_recv()
+            echunk(d, 4, sibling).start()
+
     def whole(d, kind, panel):
         rows = u.at[panel, pl.ds(d * (CB * B // 4), CB * B // 4 + ER)]
         return pltpu.make_async_remote_copy(
             src_ref=rows, dst_ref=rows, send_sem=usend.at[d, kind], recv_sem=usib.at[d], device_id=sibling)
-
-    for d in range(4):
-        whole(d, 4, other).wait_recv()
-
-    panel = lambda k: lp[k]
-    l_first = high(panel(0), gmat[0])
-    u_01 = u[0, pl.ds(EXTRA, B), :]
-    f_col = jnp.concatenate(
-        [jnp.broadcast_to(fcol[pl.ds(r, 1), :], (B, B)) for r in range(RB)], axis=0)
-    second = panel(1) - f_col * high(l_first, u_01)
-    l_second = high(second, gmat[1])
-    q10 = split(high(u[1, pl.ds(EXTRA, B), :], gmat[0]))
-    left[:, 0:B] = l_first
-    left[:, B:2 * B] = l_second
 
     @pl.loop(1, CB)
     def _(c):
         for r in range(1, RB):
             load(r, c).wait()
 
+    for d in range(4):
+        whole(d, 4, other).wait_recv()
+
+    u_01 = u[0, pl.ds(EXTRA, B), :]
+    f_col = jnp.concatenate(
+        [jnp.broadcast_to(fcol[pl.ds(r, 1), :], (B, B)) for r in range(RB)], axis=0)
+    second = panel(1) - f_col * dot3(split(l_first), split(u_01))
+    left[:, B:2 * B] = dot3(split(second), g_second)
+    q10 = split(dot3(split(u[1, pl.ds(EXTRA, B), :]), g_first))
+
     @pl.when(is_root)
     def _():
         left[pl.ds(0, B), B:2 * B] = jnp.zeros((B, B), F32)
-        own = pmat[core].T
-
-        @pl.loop(0, CB)
-        def _(c):
-            vals[0, c] = high(own, vals[0, c])
 
     @pl.when(row == 0)
     def _():
@@ -299,7 +401,7 @@
 
     @pl.when(row == 1)
     def _():
-        left[pl.ds(0, B), 0:B] = high(pmat[1].T, left[pl.ds(0, B), 0:B])
+        left[pl.ds(0, B), 0:B] = high(pmat[1], left[pl.ds(0, B), 0:B])
 
     lhs = split(left[...])
 
@@ -405,6 +507,8 @@
             pltpu.SemaphoreType.DMA((2,)),
             pltpu.SemaphoreType.DMA((NZ,)),
             pltpu.SemaphoreType.DMA(()),
+            pltpu.SemaphoreType.REGULAR((2,)),
+            pltpu.SemaphoreType.REGULAR((NZ,)),
         ],
         compiler_params=pltpu.CompilerParams(
             collective_id=0, has_side_effects=True, vmem_limit_bytes=24 << 20),

time: 43.2 us -> 42 us (0.972)
  Pallas kernels: 41.1 us -> 39.9 us
    pallas_call x1, Pallas kernels: 41.1 us -> 39.9 us  [per_device(): pl.pallas_call(kernel, out_shape=jax.ShapeDtypeStruct(shape, F32), in_spe...]
where the time goes in v3:
time: 42 us; the launch traced here: 41.9 us
  Pallas kernels  39.9 us (95%)
  local copies, waits for them, and re-layouts  2.02 us (5%)
    pallas_call x1, Pallas kernels, per_device(): pl.pallas_call(kernel, out_shape=jax.ShapeDtypeStruct(shape, F32), in_spe...  39.9 us
    unnamed x1, local copies, waits for them, and re-layouts  2.02 us

profile of v3, /device:TPU:13, one launch (start us, length us, event | category | flops | bytes accessed | tf_op | source)
XLA Modules:
  0.0 41.9 jit_solution(2368719885614534741)
XLA Ops:
  0.0 39.9 %shard_map.46 = f32[4,128,16,1,128]{4,3,2,1,0:T(1,128)S(1)} custom-call(f32[4,128,16,1,128]{4,3,2,1,0:T(1,128)} %bitcast.8, s32[4,1,16]{2,1,0:T(1,128)} %bitcast.9, f32[2,128,128]{2,1,0:T(8,128)} %inverses_hbm.1, s32[2,128]{1,0:T(2,128)} %pivots_hbm.1), custom_call_target="tpu_custom_call" | custom-call | tf_op jit(solution)/shard_map/pallas_call | solution.py:482
  39.9 2.0 %copy.8 = f32[4,1,128,16,1,128]{5,4,3,2,1,0:T(1,128)} copy(f32[4,1,128,16,1,128]{5,4,3,2,1,0:T(1,128)S(1)} %bitcast.7) | data formatting | bytes 8388608

commit v4 on v3

--- a/solution.py
+++ b/solution.py
@@ -21,9 +21,10 @@
 R = CB * B // 4 // N
 NL = 8
 RL = RB * B // NL
-LA = 4
-LB = 2
-LROOT = 8
+LA = 5
+LS = 2
+LB = 1
+LROOT = 4
 
 
 def split(x):
@@ -235,9 +236,10 @@
                     fcopy(s).start()
 
         for k, s, hops, get, give, dev in ways:
-            j = base - LA * hops
-
-            @pl.when((j >= 0) & (j < get))
+            due = base - LA * hops
+            j = jnp.maximum(due, 0) // LS
+
+            @pl.when((due >= 0) & (due % LS == 0) & (j < get))
             def _():
                 @pl.when(hops > 0)
                 def _():
@@ -334,7 +336,7 @@
         inverse_products()
         pmat[core] = pmat[core].T
 
-    @pl.loop(N, jnp.maximum(LA * (4 - weight) + start + NL, N))
+    @pl.loop(N, jnp.maximum(LA * (4 - weight) + start + LS * NL, N))
     def _(n):
         columns(n)
 
@@ -408,7 +410,7 @@
     def store(r, c):
         return pltpu.make_async_copy(vals.at[r, c], out.at[r, :, c, 0, :], out_sem.at[r, c])
 
-    @pl.loop(0, CB // 2)
+    @pl.loop(0, CB // 2, unroll=2)
     def _(j):
         c = 2 * j
         pair = lambda k: jnp.concatenate(

time: 42 us -> 41.2 us (0.981)
  Pallas kernels: 39.9 us -> 39 us
    pallas_call x1, Pallas kernels: 39.9 us -> 39 us  [per_device(): pl.pallas_call(kernel, out_shape=jax.ShapeDtypeStruct(shape, F32), in_spe...]
where the time goes in v4:
time: 41.2 us; the launch traced here: 41.1 us
  Pallas kernels  39 us (95%)
  local copies, waits for them, and re-layouts  2.02 us (5%)
    pallas_call x1, Pallas kernels, per_device(): pl.pallas_call(kernel, out_shape=jax.ShapeDtypeStruct(shape, F32), in_spe...  39 us
    unnamed x1, local copies, waits for them, and re-layouts  2.02 us

profile of v4, /device:TPU:13, one launch (start us, length us, event | category | flops | bytes accessed | tf_op | source)
XLA Modules:
  0.0 41.1 jit_solution(1731188512113639147)
XLA Ops:
  0.0 39.0 %shard_map.46 = f32[4,128,16,1,128]{4,3,2,1,0:T(1,128)S(1)} custom-call(f32[4,128,16,1,128]{4,3,2,1,0:T(1,128)} %bitcast.8, s32[4,1,16]{2,1,0:T(1,128)} %bitcast.9, f32[2,128,128]{2,1,0:T(8,128)} %inverses_hbm.1, s32[2,128]{1,0:T(2,128)} %pivots_hbm.1), custom_call_target="tpu_custom_call" | custom-call | tf_op jit(solution)/shard_map/pallas_call | solution.py:484
  39.1 2.0 %copy.8 = f32[4,1,128,16,1,128]{5,4,3,2,1,0:T(1,128)} copy(f32[4,1,128,16,1,128]{5,4,3,2,1,0:T(1,128)S(1)} %bitcast.7) | data formatting | bytes 8388608

commit v5 on v4

--- a/solution.py
+++ b/solution.py
@@ -21,9 +21,9 @@
 R = CB * B // 4 // N
 NL = 8
 RL = RB * B // NL
-LA = 5
+LA = 6
 LS = 2
-LB = 1
+LB = 0
 LROOT = 4
 
 

time: 41.2 us -> 41.9 us (1.017)
  Pallas kernels: 39 us -> 39.8 us
    pallas_call x1, Pallas kernels: 39 us -> 39.8 us  [per_device(): pl.pallas_call(kernel, out_shape=jax.ShapeDtypeStruct(shape, F32), in_spe...]
where the time goes in v5:
time: 41.9 us; the launch traced here: 41.8 us
  Pallas kernels  39.8 us (95%)
  local copies, waits for them, and re-layouts  2.02 us (5%)
    pallas_call x1, Pallas kernels, per_device(): pl.pallas_call(kernel, out_shape=jax.ShapeDtypeStruct(shape, F32), in_spe...  39.8 us
    unnamed x1, local copies, waits for them, and re-layouts  2.02 us

profile of v5, /device:TPU:13, one launch (start us, length us, event | category | flops | bytes accessed | tf_op | source)
XLA Modules:
  0.0 41.8 jit_solution(10551310523142966247)
XLA Ops:
  0.0 39.8 %shard_map.46 = f32[4,128,16,1,128]{4,3,2,1,0:T(1,128)S(1)} custom-call(f32[4,128,16,1,128]{4,3,2,1,0:T(1,128)} %bitcast.8, s32[4,1,16]{2,1,0:T(1,128)} %bitcast.9, f32[2,128,128]{2,1,0:T(8,128)} %inverses_hbm.1, s32[2,128]{1,0:T(2,128)} %pivots_hbm.1), custom_call_target="tpu_custom_call" | custom-call | tf_op jit(solution)/shard_map/pallas_call | solution.py:484
  39.8 2.0 %copy.8 = f32[4,1,128,16,1,128]{5,4,3,2,1,0:T(1,128)} copy(f32[4,1,128,16,1,128]{5,4,3,2,1,0:T(1,128)S(1)} %bitcast.7) | data formatting | bytes 8388608
